TPU v7x, 32 devices: a whole 2x2x4 slice. The times are simulated.
32 devices in a mesh: gx: 16 (over z, x, core), gy: 2 (over y).
Axes of the slice: x: 2, y: 2, z: 4, core: 2. Of those that a mesh axis runs over, the one named last changes fastest.
Arguments:
- queries: bfloat16 [64, 128, 1024], P('gx', 'gy'), may hold values from -42 to 42
- key_tokens: bfloat16 [64, 128, 1024], P('gx', 'gy'), may hold values from -6 to 6
- value_tokens: bfloat16 [64, 128, 1024], P('gx', 'gy'), may hold values from -6 to 6
- out_grad: bfloat16 [64, 128, 1024], P('gx', 'gy'), may hold values from -6 to 6
- conv_weight: float32 [9, 1024], replicated, may hold values from -0.9 to 0.9
- block_pairs: int32 [16, 2, 16, 2], P('gx', 'gy'), may hold values from 0 to 31, as said below
Outputs:
- layer_out: bfloat16 [64, 128, 1024], P('gx', 'gy')
- query_grad: bfloat16 [64, 128, 1024], P('gx', 'gy')
- key_grad: bfloat16 [64, 128, 1024], P('gx', 'gy')
- value_grad: bfloat16 [64, 128, 1024], P('gx', 'gy')
Inputs may be any that keep to these rules, and one draw needn't show every extreme that they name: block_pairs[i, j, p] = (a local query block of tile (i, j), below 2; a key block of column j, which lies on tile (key block) // 2 along the first dimension). That tile is i + o modulo 16 with o one of 0, 1, -1, 4, 8, 12. Pairs may repeat.
All inputs are finite; a program needn't handle non-finite values.
Results may differ from a plain program's by a relative error of at most 0.009.
Values may be sent and summed in bfloat16 or wider, within the bound.
A program may use at most 128 MiB of HBM per device.

v0:
```python
from functools import partial
import math

import jax
import jax.numpy as jnp
from jax import lax
from jax.sharding import PartitionSpec as P

HD = 128
BLOCK = 128


lowest_score = -1e30


def extended(x, sides, width):
    for axis, dim in sides:
        size, length = (lax.axis_size(axis), x.shape[dim])
        up = [(i, (i + 1) % size) for i in range(size - 1)]
        down = [(j, i) for i, j in up]
        last = lax.slice_in_dim(x, length - width, length, axis=dim)
        leading = lax.slice_in_dim(x, 0, width, axis=dim)
        before = lax.ppermute(last, axis, up)
        after = lax.ppermute(leading, axis, down)
        x = jnp.concatenate([before, x, after], axis=dim)
    return x


def passed_along(value, axis, steps):
    count = lax.axis_size(axis)
    pairs = [(source, (source + steps) % count) for source in range(count)]
    return lax.ppermute(value, axis, pairs)


def head_view(tile_data):
    flat = tile_data.reshape(-1, tile_data.shape[-1])
    return flat.reshape(flat.shape[0], -1, HD)


def stencil(padded, weights, direction, row_count, col_count):
    running_sum = jnp.zeros((row_count, col_count, padded.shape[2]), jnp.float32)
    for row_step in (-1, 0, 1):
        for col_step in (-1, 0, 1):
            row_first = 1 + direction * row_step
            col_first = 1 + direction * col_step
            window = padded[row_first : row_first + row_count, col_first : col_first + col_count]
            running_sum = running_sum + weights[3 * (row_step + 1) + col_step + 1] * window
    return running_sum


def block_mask(block_pairs, query_tile, key_tile, block_count):
    listed_query = block_pairs[0, 0, :, 0]
    listed_key = block_pairs[0, 0, :, 1]
    local_blocks = jnp.arange(block_count, dtype=jnp.int32)
    wanted = key_tile * block_count + local_blocks
    listed = (listed_query[:, None, None] == local_blocks[None, :, None]) & (
        listed_key[:, None, None] == wanted[None, None, :]
    )
    diagonal = (query_tile == key_tile) & (local_blocks[:, None] == local_blocks[None, :])
    return jnp.any(listed, axis=0) | diagonal


def raw_scores(query_heads, key_heads):
    return jnp.einsum(
        "qhd,khd->hqk", query_heads, key_heads, preferred_element_type=jnp.float32
    ) * (1.0 / math.sqrt(HD))


def visible_of(allowed, head_count, nquery, key_count):
    shaped = (head_count, nquery // BLOCK, BLOCK, key_count // BLOCK, BLOCK)
    return jnp.broadcast_to(allowed[None, :, None, :, None], shaped).reshape(
        head_count, nquery, key_count
    )


def stats_update(score_source, allowed, totals):
    scores = score_source()
    visible = visible_of(allowed, *scores.shape)
    old_max, old_sum = totals
    new_max = jnp.maximum(old_max, jnp.max(jnp.where(visible, scores, lowest_score), axis=2))
    fresh = jnp.sum(jnp.where(visible, jnp.exp(scores - new_max[:, :, None]), 0.0), axis=2)
    return (new_max, old_sum * jnp.exp(old_max - new_max) + fresh)


def output_update(score_source, value_piece, allowed, log_total, totals):
    scores = score_source()
    visible = visible_of(allowed, *scores.shape)
    weights = jnp.where(visible, jnp.exp(scores - log_total[:, :, None]), 0.0).astype(jnp.bfloat16)
    return totals + jnp.einsum(
        "hqk,khd->qhd", weights, value_piece, preferred_element_type=jnp.float32
    )


def query_update(
    score_source,
    query_heads,
    grad_heads,
    log_total,
    grad_dot,
    key_piece,
    value_piece,
    allowed,
    with_parts,
    totals,
):
    scores = score_source()
    visible = visible_of(allowed, *scores.shape)
    probabilities = jnp.where(visible, jnp.exp(scores - log_total[:, :, None]), 0.0)
    prob_grad = jnp.einsum(
        "qhd,khd->hqk", grad_heads, value_piece, preferred_element_type=jnp.float32
    )
    score_grad = (
        probabilities * (prob_grad - grad_dot[:, :, None]) * (1.0 / math.sqrt(HD))
    ).astype(jnp.bfloat16)
    dquery = totals[0] + jnp.einsum(
        "hqk,khd->qhd", score_grad, key_piece, preferred_element_type=jnp.float32
    )
    key_part = jnp.einsum(
        "hqk,qhd->khd", score_grad, query_heads, preferred_element_type=jnp.float32
    )
    value_part = jnp.einsum(
        "hqk,qhd->khd",
        probabilities.astype(jnp.bfloat16),
        grad_heads,
        preferred_element_type=jnp.float32,
    )
    return (dquery, key_part, value_part)


def per_device(queries, key_tokens, value_tokens, out_grad, conv_weight, block_pairs):
    cycle_size = lax.axis_size("gx")
    own_tile = lax.axis_index("gx")
    tile_x, tile_y, width = queries.shape
    token_count = tile_x * tile_y
    block_count = token_count // BLOCK
    head_count = width // HD
    quarter = cycle_size // 4
    offsets = [0, 1, cycle_size - 1, quarter, 2 * quarter, 3 * quarter]
    query_heads = head_view(queries)
    key_heads = head_view(key_tokens)
    value_heads = head_view(value_tokens)
    grad_heads = head_view(out_grad)
    allows = [
        block_mask(block_pairs, own_tile, (own_tile + offset) % cycle_size, block_count)
        for offset in offsets
    ]
    value_pad = extended(value_tokens, (("gx", 0), ("gy", 1)), 1)
    conv_value = stencil(value_pad, conv_weight, 1, tile_x, tile_y)
    kept_pieces = [(key_heads, value_heads)]
    for offset in offsets[1:]:
        arrived = passed_along((key_tokens, value_tokens), "gx", cycle_size - offset)
        kept_pieces.append((head_view(arrived[0]), head_view(arrived[1])))
    sources = [
        partial(raw_scores, query_heads, key_piece) for key_piece, value_piece in kept_pieces
    ]
    running = (
        jnp.full((head_count, token_count), lowest_score, jnp.float32),
        jnp.zeros((head_count, token_count), jnp.float32),
    )
    for source, allowed in zip(sources, allows):
        running = stats_update(source, allowed, running)
    log_total = running[0] + jnp.log(running[1])
    attended = jnp.zeros((token_count, head_count, HD), jnp.float32)
    for source, (key_piece, value_piece), allowed in zip(sources, kept_pieces, allows):
        attended = output_update(source, value_piece, allowed, log_total, attended)
    layer_out = (attended.reshape(tile_x, tile_y, width) + conv_value).astype(jnp.bfloat16)
    grad_dot = jnp.einsum("qhd,qhd->hq", grad_heads.astype(jnp.float32), attended)
    zero_heads = jnp.zeros((token_count, head_count, HD), jnp.float32)
    dquery = zero_heads
    key_sum = zero_heads
    value_sum = zero_heads
    for slot_index, (source, (key_piece, value_piece), allowed) in enumerate(
        zip(sources, kept_pieces, allows)
    ):
        update = partial(
            query_update,
            source,
            query_heads,
            grad_heads,
            log_total,
            grad_dot,
            key_piece,
            value_piece,
            allowed,
            True,
        )
        results = update((dquery, zero_heads, zero_heads))
        dquery = results[0]
        if slot_index == 0:
            key_sum = results[1]
            value_sum = results[2]
        else:
            partials = passed_along((results[1], results[2]), "gx", offsets[slot_index])
            key_sum = key_sum + partials[0]
            value_sum = value_sum + partials[1]
    grad_pad = extended(out_grad, (("gx", 0), ("gy", 1)), 1)
    conv_back = stencil(grad_pad, conv_weight, -1, tile_x, tile_y)
    query_grad = dquery.reshape(tile_x, tile_y, width).astype(jnp.bfloat16)
    key_grad = key_sum.reshape(tile_x, tile_y, width).astype(jnp.bfloat16)
    value_grad = (value_sum.reshape(tile_x, tile_y, width) + conv_back).astype(jnp.bfloat16)
    return (layer_out, query_grad, key_grad, value_grad)


def solution(mesh):
    return jax.shard_map(
        per_device,
        mesh=mesh,
        in_specs=(
            P("gx", "gy", None),
            P("gx", "gy", None),
            P("gx", "gy", None),
            P("gx", "gy", None),
            P(),
            P("gx", "gy", None, None),
        ),
        out_specs=(
            P("gx", "gy", None),
            P("gx", "gy", None),
            P("gx", "gy", None),
            P("gx", "gy", None),
        ),
        check_vma=False,
    )
```

profile of v0, /device:TPU:15, one launch (start us, length us, event | category | flops | bytes accessed | tf_op | source)
XLA Modules:
  0.0 365.8 jit_solution(8870456665061685311)
XLA Ops:
  4.5 1.7 fusion.100
  6.2 3.2 collective-permute-start.24
  9.4 1.7 fusion.101
  11.1 1.9 collective-permute-start.10
  22.5 26.7 %collective-permute-done.24 = bf16[1,64,1024]{2,1,0:T(8,128)(2,1)} collective-permute-done((bf16[1,64,1024]{2,1,0:T(8,128)(2,1)}, bf16[1,64,1024]{2,1,0:T(8,128)(2,1)}, u32[]{:S(2)}, u32[]{:S(2)}) %collective-permute-start.24) | collective-permute-done | bytes 131104 | tf_op jit(solution)/shard_map/ppermute | solution.py:23
  49.2 3.4 collective-permute-start.1
  53.5 1.9 collective-permute-start.25
  56.4 4.3 %collective-permute-done.25 = bf16[1,64,1024]{2,1,0:T(8,128)(2,1)S(1)} collective-permute-done((bf16[1,64,1024]{2,1,0:T(8,128)(2,1)S(1)}, bf16[1,64,1024]{2,1,0:T(8,128)(2,1)S(1)}, u32[]{:S(2)}, u32[]{:S(2)}) %collective-permute-start.25) | collective-permute-done | bytes 131104 | tf_op jit(solution)/shard_map/ppermute | solution.py:24
  60.7 1.9 collective-permute-start.11
  62.7 5.3 %collective-permute-done.11 = bf16[1,64,1024]{2,1,0:T(8,128)(2,1)S(1)} collective-permute-done((bf16[1,64,1024]{2,1,0:T(8,128)(2,1)S(1)}, bf16[1,64,1024]{2,1,0:T(8,128)(2,1)S(1)}, u32[]{:S(2)}, u32[]{:S(2)}) %collective-permute-start.11) | collective-permute-done | bytes 131104 | tf_op jit(solution)/shard_map/ppermute | solution.py:24
  68.1 2.6 collective-permute-start.6
  76.2 3.1 collective-permute-done
  79.5 33.6 %collective-permute-done.5 = bf16[4,64,1024]{2,1,0:T(8,128)(2,1)S(1)} collective-permute-done((bf16[4,64,1024]{2,1,0:T(8,128)(2,1)S(1)}, bf16[4,64,1024]{2,1,0:T(8,128)(2,1)S(1)}, u32[]{:S(2)}, u32[]{:S(2)}) %collective-permute-start.5) | collective-permute-done | bytes 524320 | tf_op jit(solution)/shard_map/ppermute | solution.py:32
  114.5 5.4 %collective-permute-start.13 = (bf16[6,1,1024]{2,1,0:T(2,128)(2,1)}, bf16[6,1,1024]{2,1,0:T(2,128)(2,1)}, u32[]{:S(2)}, u32[]{:S(2)}) collective-permute-start(bf16[6,1,1024]{2,1,0:T(2,128)(2,1)} %get-tuple-element.18), channel_id=1, source_target_pairs={{1,0},{3,2},{5,4},{7,6},{9,8},{11,10},{13,12},{15,14},{17,16},{19,... | collective-permute-start | bytes 36872 | tf_op jit(solution)/shard_map/ppermute | solution.py:24
  125.6 1.6 convolution_bitcast_fusion.4
  127.1 1.6 convolution_bitcast_fusion.3
  132.1 1.6 convolution_bitcast_fusion
  140.1 2.6 multiply_convert_fusion
  164.1 9.6 %collective-permute-done.19 = f32[256,8,128]{2,0,1:T(8,128)S(1)} collective-permute-done((f32[256,8,128]{2,0,1:T(8,128)S(1)}, f32[256,8,128]{2,0,1:T(8,128)S(1)}, u32[]{:S(2)}, u32[]{:S(2)}) %collective-permute-start.19) | collective-permute-done | bytes 1048608 | tf_op jit(solution)/shard_map/ppermute | solution.py:32
  173.7 46.7 %collective-permute-done.20 = f32[256,8,128]{2,0,1:T(8,128)S(1)} collective-permute-done((f32[256,8,128]{2,0,1:T(8,128)S(1)}, f32[256,8,128]{2,0,1:T(8,128)S(1)}, u32[]{:S(2)}, u32[]{:S(2)}) %collective-permute-start.20) | collective-permute-done | bytes 1048608 | tf_op jit(solution)/shard_map/ppermute | solution.py:32
  220.4 65.7 %collective-permute-done.21 = f32[256,8,128]{2,0,1:T(8,128)S(1)} collective-permute-done((f32[256,8,128]{2,0,1:T(8,128)S(1)}, f32[256,8,128]{2,0,1:T(8,128)S(1)}, u32[]{:S(2)}, u32[]{:S(2)}) %collective-permute-start.21) | collective-permute-done | bytes 1048608 | tf_op jit(solution)/shard_map/ppermute | solution.py:32
  286.1 2.3 collective-permute-start.16
  288.4 20.2 %collective-permute-done.22 = f32[256,8,128]{2,0,1:T(8,128)S(1)} collective-permute-done((f32[256,8,128]{2,0,1:T(8,128)S(1)}, f32[256,8,128]{2,0,1:T(8,128)S(1)}, u32[]{:S(2)}, u32[]{:S(2)}) %collective-permute-start.22) | collective-permute-done | bytes 1048608 | tf_op jit(solution)/shard_map/ppermute | solution.py:32
  308.6 2.9 collective-permute-start.14
  313.5 1.6 copy.162
  316.5 3.6 add_convert_fusion.1
  320.2 3.0 fusion.10
  324.6 6.6 %collective-permute-done.17 = f32[256,8,128]{2,0,1:T(8,128)} collective-permute-done((f32[256,8,128]{2,0,1:T(8,128)}, f32[256,8,128]{2,0,1:T(8,128)}, u32[]{:S(2)}, u32[]{:S(2)}) %collective-permute-start.17) | collective-permute-done | bytes 1048608 | tf_op jit(solution)/shard_map/ppermute | solution.py:32
  332.5 10.3 %collective-permute-done.16 = f32[256,8,128]{2,0,1:T(8,128)} collective-permute-done((f32[256,8,128]{2,0,1:T(8,128)}, f32[256,8,128]{2,0,1:T(8,128)}, u32[]{:S(2)}, u32[]{:S(2)}) %collective-permute-start.16) | collective-permute-done | bytes 1048608 | tf_op jit(solution)/shard_map/ppermute | solution.py:32
  342.8 13.2 %collective-permute-done.15 = f32[256,8,128]{2,0,1:T(8,128)} collective-permute-done((f32[256,8,128]{2,0,1:T(8,128)}, f32[256,8,128]{2,0,1:T(8,128)}, u32[]{:S(2)}, u32[]{:S(2)}) %collective-permute-start.15) | collective-permute-done | bytes 1048608 | tf_op jit(solution)/shard_map/ppermute | solution.py:32
  355.9 3.0 fusion.16
  361.1 4.2 %add_convert_fusion = bf16[4,64,1024]{2,1,0:T(8,128)(2,1)} fusion(f32[4,64,1024]{2,1,0:T(8,128)S(1)} %reshape.467, bf16[4,64,1024]{2,1,0:T(8,128)(2,1)S(1)} %copy-done.14, bf16[6,64,1024]{2,1,0:T(8,128)(2,1)} %copy-done.41, bf16[6,1,1024]{2,1,0:T(2,128)(2,1)S(1)} %collective-permute-done.27, bf16[6,1,1024]{2,1,0:T(2,128)(2,1)S(1)} %collective-permute-done.26, ...), kind=kLoop, calls=%fused_computation.74 | loop fusion | flops 13631488 | bytes 3207168 | tf_op jit(solution)/shard_map/convert_element_type | solution.py:200
  (286 shorter events, 66.3 us)
Async XLA Ops:
  0.7 67.4 %collective-permute-start.4 = (bf16[4,64,1024]{2,1,0:T(8,128)(2,1)}, bf16[4,64,1024]{2,1,0:T(8,128)(2,1)}, u32[]{:S(2)}, u32[]{:S(2)}) collective-permute-start(bf16[4,64,1024]{2,1,0:T(8,128)(2,1)} %param.7), channel_id=1, source_target_pairs={{0,8},{2,10},{4,12},{6,14},{8,16},{10,18},{12,20},{14,22},{16,24},... | collective-permute-start | bytes 1572872 | tf_op jit(solution)/shard_map/ppermute | solution.py:32
  2.0 66.1 %collective-permute-start.3 = (bf16[4,64,1024]{2,1,0:T(8,128)(2,1)}, bf16[4,64,1024]{2,1,0:T(8,128)(2,1)}, u32[]{:S(2)}, u32[]{:S(2)}) collective-permute-start(bf16[4,64,1024]{2,1,0:T(8,128)(2,1)} %param.7), channel_id=1, source_target_pairs={{0,16},{2,18},{4,20},{6,22},{8,24},{10,26},{12,28},{14,30},{16,0},... | collective-permute-start | bytes 1572872 | tf_op jit(solution)/shard_map/ppermute | solution.py:32
  3.1 71.6 %collective-permute-start.2 = (bf16[4,64,1024]{2,1,0:T(8,128)(2,1)}, bf16[4,64,1024]{2,1,0:T(8,128)(2,1)}, u32[]{:S(2)}, u32[]{:S(2)}) collective-permute-start(bf16[4,64,1024]{2,1,0:T(8,128)(2,1)} %param.7), channel_id=1, source_target_pairs={{0,24},{2,26},{4,28},{6,30},{8,0},{10,2},{12,4},{14,6},{16,8},{18,... | collective-permute-start | bytes 1572872 | tf_op jit(solution)/shard_map/ppermute | solution.py:32
  6.2 43.0 %collective-permute-start.24 = (bf16[1,64,1024]{2,1,0:T(8,128)(2,1)}, bf16[1,64,1024]{2,1,0:T(8,128)(2,1)}, u32[]{:S(2)}, u32[]{:S(2)}) collective-permute-start(bf16[1,64,1024]{2,1,0:T(8,128)(2,1)} %get-tuple-element.20), channel_id=1, source_target_pairs={{0,2},{2,4},{4,6},{6,8},{8,10},{10,12},{12,14},{14,16},{16,18},{18... | collective-permute-start | bytes 393224 | tf_op jit(solution)/shard_map/ppermute | solution.py:23
  11.1 42.5 %collective-permute-start.10 = (bf16[1,64,1024]{2,1,0:T(8,128)(2,1)}, bf16[1,64,1024]{2,1,0:T(8,128)(2,1)}, u32[]{:S(2)}, u32[]{:S(2)}) collective-permute-start(bf16[1,64,1024]{2,1,0:T(8,128)(2,1)} %get-tuple-element.22), channel_id=1, source_target_pairs={{0,2},{2,4},{4,6},{6,8},{8,10},{10,12},{12,14},{14,16},{16,18},{18... | collective-permute-start | bytes 393224 | tf_op jit(solution)/shard_map/ppermute | solution.py:23
  17.8 115.8 %copy-start = (f32[8,256,256]{1,2,0:T(8,128)}, f32[8,256,256]{1,2,0:T(8,128)S(1)}, u32[]{:S(2)}) copy-start(f32[8,256,256]{1,2,0:T(8,128)S(1)} %get-tuple-element.52) | copy-start | bytes 6291460
  22.4 116.4 %copy-start.15 = (bf16[32,8,8,128]{3,2,1,0:T(8,128)(2,1)}, bf16[32,8,8,128]{3,2,1,0:T(8,128)(2,1)S(1)}, u32[]{:S(2)}) copy-start(bf16[32,8,8,128]{3,2,1,0:T(8,128)(2,1)S(1)} %copy.252) | copy-start | bytes 1572868
  49.2 26.8 %collective-permute-start.1 = (bf16[4,64,1024]{2,1,0:T(8,128)(2,1)S(1)}, bf16[4,64,1024]{2,1,0:T(8,128)(2,1)S(1)}, u32[]{:S(2)}, u32[]{:S(2)}) collective-permute-start(bf16[4,64,1024]{2,1,0:T(8,128)(2,1)S(1)} %copy-done.52), channel_id=1, source_target_pairs={{0,2},{2,4},{4,6},{6,8},{8,10},{10,12},{12,14},{14,16},{16,18},{18... | collective-permute-start | bytes 1572872 | tf_op jit(solution)/shard_map/ppermute | solution.py:32
  53.5 7.2 %collective-permute-start.25 = (bf16[1,64,1024]{2,1,0:T(8,128)(2,1)S(1)}, bf16[1,64,1024]{2,1,0:T(8,128)(2,1)S(1)}, u32[]{:S(2)}, u32[]{:S(2)}) collective-permute-start(bf16[1,64,1024]{2,1,0:T(8,128)(2,1)S(1)} %copy-done.56), channel_id=1, source_target_pairs={{2,0},{4,2},{6,4},{8,6},{10,8},{12,10},{14,12},{16,14},{18,16},{20... | collective-permute-start | bytes 393224 | tf_op jit(solution)/shard_map/ppermute | solution.py:24
  60.7 7.3 %collective-permute-start.11 = (bf16[1,64,1024]{2,1,0:T(8,128)(2,1)S(1)}, bf16[1,64,1024]{2,1,0:T(8,128)(2,1)S(1)}, u32[]{:S(2)}, u32[]{:S(2)}) collective-permute-start(bf16[1,64,1024]{2,1,0:T(8,128)(2,1)S(1)} %copy-done.55), channel_id=1, source_target_pairs={{2,0},{4,2},{6,4},{8,6},{10,8},{12,10},{14,12},{16,14},{18,16},{20... | collective-permute-start | bytes 393224 | tf_op jit(solution)/shard_map/ppermute | solution.py:24
  68.0 11.4 %collective-permute-start = (bf16[4,64,1024]{2,1,0:T(8,128)(2,1)S(1)}, bf16[4,64,1024]{2,1,0:T(8,128)(2,1)S(1)}, u32[]{:S(2)}, u32[]{:S(2)}) collective-permute-start(bf16[4,64,1024]{2,1,0:T(8,128)(2,1)S(1)} %copy-done.52), channel_id=1, source_target_pairs={{0,30},{2,0},{4,2},{6,4},{8,6},{10,8},{12,10},{14,12},{16,14},{18,... | collective-permute-start | bytes 1572872 | tf_op jit(solution)/shard_map/ppermute | solution.py:32
  68.0 45.1 %collective-permute-start.5 = (bf16[4,64,1024]{2,1,0:T(8,128)(2,1)S(1)}, bf16[4,64,1024]{2,1,0:T(8,128)(2,1)S(1)}, u32[]{:S(2)}, u32[]{:S(2)}) collective-permute-start(bf16[4,64,1024]{2,1,0:T(8,128)(2,1)S(1)} %copy-done.12), channel_id=1, source_target_pairs={{0,30},{2,0},{4,2},{6,4},{8,6},{10,8},{12,10},{14,12},{16,14},{18,... | collective-permute-start | bytes 1572872 | tf_op jit(solution)/shard_map/ppermute | solution.py:32
  68.1 46.4 %collective-permute-start.6 = (bf16[4,64,1024]{2,1,0:T(8,128)(2,1)S(1)}, bf16[4,64,1024]{2,1,0:T(8,128)(2,1)S(1)}, u32[]{:S(2)}, u32[]{:S(2)}) collective-permute-start(bf16[4,64,1024]{2,1,0:T(8,128)(2,1)S(1)} %copy-done.12), channel_id=1, source_target_pairs={{0,2},{2,4},{4,6},{6,8},{8,10},{10,12},{12,14},{14,16},{16,18},{18... | collective-permute-start | bytes 1572872 | tf_op jit(solution)/shard_map/ppermute | solution.py:32
  74.7 54.1 %collective-permute-start.7 = (bf16[4,64,1024]{2,1,0:T(8,128)(2,1)S(1)}, bf16[4,64,1024]{2,1,0:T(8,128)(2,1)S(1)}, u32[]{:S(2)}, u32[]{:S(2)}) collective-permute-start(bf16[4,64,1024]{2,1,0:T(8,128)(2,1)S(1)} %copy-done.12), channel_id=1, source_target_pairs={{0,24},{2,26},{4,28},{6,30},{8,0},{10,2},{12,4},{14,6},{16,8},{18,... | collective-permute-start | bytes 1572872 | tf_op jit(solution)/shard_map/ppermute | solution.py:32
  76.0 55.9 %collective-permute-start.8 = (bf16[4,64,1024]{2,1,0:T(8,128)(2,1)S(1)}, bf16[4,64,1024]{2,1,0:T(8,128)(2,1)S(1)}, u32[]{:S(2)}, u32[]{:S(2)}) collective-permute-start(bf16[4,64,1024]{2,1,0:T(8,128)(2,1)S(1)} %copy-done.12), channel_id=1, source_target_pairs={{0,16},{2,18},{4,20},{6,22},{8,24},{10,26},{12,28},{14,30},{16,0},... | collective-permute-start | bytes 1572872 | tf_op jit(solution)/shard_map/ppermute | solution.py:32
  79.4 55.0 %collective-permute-start.9 = (bf16[4,64,1024]{2,1,0:T(8,128)(2,1)S(1)}, bf16[4,64,1024]{2,1,0:T(8,128)(2,1)S(1)}, u32[]{:S(2)}, u32[]{:S(2)}) collective-permute-start(bf16[4,64,1024]{2,1,0:T(8,128)(2,1)S(1)} %copy-done.12), channel_id=1, source_target_pairs={{0,8},{2,10},{4,12},{6,14},{8,16},{10,18},{12,20},{14,22},{16,24},... | collective-permute-start | bytes 1572872 | tf_op jit(solution)/shard_map/ppermute | solution.py:32
  113.1 45.0 %collective-permute-start.12 = (bf16[6,1,1024]{2,1,0:T(2,128)(2,1)}, bf16[6,1,1024]{2,1,0:T(2,128)(2,1)}, u32[]{:S(2)}, u32[]{:S(2)}) collective-permute-start(bf16[6,1,1024]{2,1,0:T(2,128)(2,1)} %get-tuple-element.17), channel_id=1, source_target_pairs={{0,1},{2,3},{4,5},{6,7},{8,9},{10,11},{12,13},{14,15},{16,17},{18,... | collective-permute-start | bytes 36872 | tf_op jit(solution)/shard_map/ppermute | solution.py:23
  114.5 43.6 %collective-permute-start.13 = (bf16[6,1,1024]{2,1,0:T(2,128)(2,1)}, bf16[6,1,1024]{2,1,0:T(2,128)(2,1)}, u32[]{:S(2)}, u32[]{:S(2)}) collective-permute-start(bf16[6,1,1024]{2,1,0:T(2,128)(2,1)} %get-tuple-element.18), channel_id=1, source_target_pairs={{1,0},{3,2},{5,4},{7,6},{9,8},{11,10},{13,12},{15,14},{17,16},{19,... | collective-permute-start | bytes 36872 | tf_op jit(solution)/shard_map/ppermute | solution.py:24
  150.7 23.0 %collective-permute-start.19 = (f32[256,8,128]{2,0,1:T(8,128)S(1)}, f32[256,8,128]{2,0,1:T(8,128)S(1)}, u32[]{:S(2)}, u32[]{:S(2)}) collective-permute-start(f32[256,8,128]{2,0,1:T(8,128)S(1)} %copy-done.73), channel_id=1, source_target_pairs={{0,2},{2,4},{4,6},{6,8},{8,10},{10,12},{12,14},{14,16},{16,18},{18... | collective-permute-start | bytes 3145736 | tf_op jit(solution)/shard_map/ppermute | solution.py:32
  151.1 69.3 %collective-permute-start.20 = (f32[256,8,128]{2,0,1:T(8,128)S(1)}, f32[256,8,128]{2,0,1:T(8,128)S(1)}, u32[]{:S(2)}, u32[]{:S(2)}) collective-permute-start(f32[256,8,128]{2,0,1:T(8,128)S(1)} %copy-done.72), channel_id=1, source_target_pairs={{0,30},{2,0},{4,2},{6,4},{8,6},{10,8},{12,10},{14,12},{16,14},{18,... | collective-permute-start | bytes 3145736 | tf_op jit(solution)/shard_map/ppermute | solution.py:32
  151.3 134.7 %collective-permute-start.21 = (f32[256,8,128]{2,0,1:T(8,128)S(1)}, f32[256,8,128]{2,0,1:T(8,128)S(1)}, u32[]{:S(2)}, u32[]{:S(2)}) collective-permute-start(f32[256,8,128]{2,0,1:T(8,128)S(1)} %copy-done.71), channel_id=1, source_target_pairs={{0,8},{2,10},{4,12},{6,14},{8,16},{10,18},{12,20},{14,22},{16,24},... | collective-permute-start | bytes 3145736 | tf_op jit(solution)/shard_map/ppermute | solution.py:32
  158.1 150.5 %collective-permute-start.22 = (f32[256,8,128]{2,0,1:T(8,128)S(1)}, f32[256,8,128]{2,0,1:T(8,128)S(1)}, u32[]{:S(2)}, u32[]{:S(2)}) collective-permute-start(f32[256,8,128]{2,0,1:T(8,128)S(1)} %copy-done.70), channel_id=1, source_target_pairs={{0,16},{2,18},{4,20},{6,22},{8,24},{10,26},{12,28},{14,30},{16,0},... | collective-permute-start | bytes 3145736 | tf_op jit(solution)/shard_map/ppermute | solution.py:32
  158.6 150.1 %collective-permute-start.23 = (f32[256,8,128]{2,0,1:T(8,128)S(1)}, f32[256,8,128]{2,0,1:T(8,128)S(1)}, u32[]{:S(2)}, u32[]{:S(2)}) collective-permute-start(f32[256,8,128]{2,0,1:T(8,128)S(1)} %copy-done.69), channel_id=1, source_target_pairs={{0,24},{2,26},{4,28},{6,30},{8,0},{10,2},{12,4},{14,6},{16,8},{18,... | collective-permute-start | bytes 3145736 | tf_op jit(solution)/shard_map/ppermute | solution.py:32
  163.6 147.9 %copy-start.38 = (bf16[32,8,8,128]{3,2,1,0:T(8,128)(2,1)S(1)}, bf16[32,8,8,128]{3,2,1,0:T(8,128)(2,1)}, u32[]{:S(2)}) copy-start(bf16[32,8,8,128]{3,2,1,0:T(8,128)(2,1)} %copy-done.37) | copy-start | bytes 1572868
  173.7 138.3 %copy-start.42 = (f32[256,8,128]{2,0,1:T(8,128)}, f32[256,8,128]{2,0,1:T(8,128)S(1)}, u32[]{:S(2)}) copy-start(f32[256,8,128]{2,0,1:T(8,128)S(1)} %collective-permute-done.19) | copy-start | bytes 3145732
  173.7 149.5 %collective-permute-start.18 = (f32[256,8,128]{2,0,1:T(8,128)}, f32[256,8,128]{2,0,1:T(8,128)}, u32[]{:S(2)}, u32[]{:S(2)}) collective-permute-start(f32[256,8,128]{2,0,1:T(8,128)} %convolution_bitcast_fusion.6), channel_id=1, source_target_pairs={{0,24},{2,26},{4,28},{6,30},{8,0},{10,2},{12,4},{14,6},{16,8},{18,... | collective-permute-start | bytes 3145736 | tf_op jit(solution)/shard_map/ppermute | solution.py:32
  220.4 110.8 %collective-permute-start.17 = (f32[256,8,128]{2,0,1:T(8,128)}, f32[256,8,128]{2,0,1:T(8,128)}, u32[]{:S(2)}, u32[]{:S(2)}) collective-permute-start(f32[256,8,128]{2,0,1:T(8,128)} %convolution_bitcast_fusion.7), channel_id=1, source_target_pairs={{0,16},{2,18},{4,20},{6,22},{8,24},{10,26},{12,28},{14,30},{16,0},... | collective-permute-start | bytes 3145736 | tf_op jit(solution)/shard_map/ppermute | solution.py:32
  286.1 56.7 %collective-permute-start.16 = (f32[256,8,128]{2,0,1:T(8,128)}, f32[256,8,128]{2,0,1:T(8,128)}, u32[]{:S(2)}, u32[]{:S(2)}) collective-permute-start(f32[256,8,128]{2,0,1:T(8,128)} %convolution_bitcast_fusion.8), channel_id=1, source_target_pairs={{0,8},{2,10},{4,12},{6,14},{8,16},{10,18},{12,20},{14,22},{16,24},... | collective-permute-start | bytes 3145736 | tf_op jit(solution)/shard_map/ppermute | solution.py:32
  308.6 47.3 %collective-permute-start.15 = (f32[256,8,128]{2,0,1:T(8,128)}, f32[256,8,128]{2,0,1:T(8,128)}, u32[]{:S(2)}, u32[]{:S(2)}) collective-permute-start(f32[256,8,128]{2,0,1:T(8,128)} %convolution_bitcast_fusion.9), channel_id=1, source_target_pairs={{0,30},{2,0},{4,2},{6,4},{8,6},{10,8},{12,10},{14,12},{16,14},{18,... | collective-permute-start | bytes 3145736 | tf_op jit(solution)/shard_map/ppermute | solution.py:32
  308.6 47.3 %collective-permute-start.14 = (f32[256,8,128]{2,0,1:T(8,128)}, f32[256,8,128]{2,0,1:T(8,128)}, u32[]{:S(2)}, u32[]{:S(2)}) collective-permute-start(f32[256,8,128]{2,0,1:T(8,128)} %convolution_bitcast_fusion.10), channel_id=1, source_target_pairs={{0,2},{2,4},{4,6},{6,8},{8,10},{10,12},{12,14},{14,16},{16,18},{18... | collective-permute-start | bytes 3145736 | tf_op jit(solution)/shard_map/ppermute | solution.py:32
  323.3 37.9 %collective-permute-start.26 = (bf16[6,1,1024]{2,1,0:T(2,128)(2,1)S(1)}, bf16[6,1,1024]{2,1,0:T(2,128)(2,1)S(1)}, u32[]{:S(2)}, u32[]{:S(2)}) collective-permute-start(bf16[6,1,1024]{2,1,0:T(2,128)(2,1)S(1)} %copy-done.66), channel_id=1, source_target_pairs={{1,0},{3,2},{5,4},{7,6},{9,8},{11,10},{13,12},{15,14},{17,16},{19,... | collective-permute-start | bytes 36872 | tf_op jit(solution)/shard_map/ppermute | solution.py:24
  331.2 29.9 %collective-permute-start.27 = (bf16[6,1,1024]{2,1,0:T(2,128)(2,1)S(1)}, bf16[6,1,1024]{2,1,0:T(2,128)(2,1)S(1)}, u32[]{:S(2)}, u32[]{:S(2)}) collective-permute-start(bf16[6,1,1024]{2,1,0:T(2,128)(2,1)S(1)} %copy-done.65), channel_id=1, source_target_pairs={{0,1},{2,3},{4,5},{6,7},{8,9},{10,11},{12,13},{14,15},{16,17},{18,... | collective-permute-start | bytes 36872 | tf_op jit(solution)/shard_map/ppermute | solution.py:23
  (70 other events, 928.9 us)
where the time goes:
time: 371 us; the launch traced here: 366 us
  waiting for transfers between devices  245 us (66%)
  matrix products  39.2 us (11%)
  starting transfers between devices  35.4 us (10%)
  local copies, waits for them, and re-layouts  31.6 us (9%)
  other arithmetic  11.7 us (3%)
    ppermute x20, waiting for transfers between devices, passed_along(): return lax.ppermute(value, axis, pairs)  209 us
    ppermute x4, waiting for transfers between devices, extended(): before = lax.ppermute(last, axis, up)  26.7 us
    ppermute x20, starting transfers between devices, passed_along(): return lax.ppermute(value, axis, pairs)  17.2 us
    unnamed x172, local copies, waits for them, and re-layouts  15.5 us
    dot_general x6, matrix products, query_update(): jnp.einsum('hqk,qhd->khd', probabilities.astype(jnp.bfloat16), grad_heads...  10.8 us
    ppermute x4, starting transfers between devices, extended(): after = lax.ppermute(leading, axis, down)  10.5 us
    dot_general x6, matrix products, query_update(): jnp.einsum('hqk,qhd->khd', score_grad, query_heads, preferred_element_typ...  10.1 us
    ppermute x4, waiting for transfers between devices, extended(): after = lax.ppermute(leading, axis, down)  9.57 us
  transfers between devices with their start and end apart: 28, of which 12 were waited for; matrix products, arithmetic and copies ran while one was open for 20% of the time, Pallas kernels for 0%

commit v1 on v0

v1 whole, which is shorter than its diff:
```python
import functools
import math

import jax
import jax.numpy as jnp
from jax import lax
from jax.experimental import pallas as pl
from jax.experimental.pallas import tpu as pltpu
from jax.sharding import PartitionSpec as P

HD = 128
BLOCK = 128
NEG = -1e30
MESH = pl.DeviceIdType.MESH
SCALE = 1.0 / math.sqrt(HD)
LOG2E = math.log2(math.e)
F32 = jnp.float32
BF16 = jnp.bfloat16


def kernel(
    n, m, tx, ty,
    q_ref, k_ref, v_ref, g_ref, w_ref, bias_ref,
    o_ref, dq_ref, dk_ref, dv_ref,
    qg, gg, kk, vv, bias_g, s_sc, dk_acc, dv_acc,
    part_send, part_recv, res, ret, edge, slab, conv,
    send_sem, recv_sem, local_sem,
):
    tokens = tx * ty
    heads = q_ref.shape[2] // HD
    hp = heads // 4
    quarter = n // 4
    own = lax.axis_index("gx")
    col = lax.axis_index("gy")
    slot = own // quarter
    rank = lax.rem(own, quarter)

    def far(d):
        return {"gx": lax.rem(own + d * quarter, n)}

    next_group = {"gx": slot * quarter + lax.rem(rank + 1, quarter)}
    prev_group = {"gx": slot * quarter + lax.rem(rank + quarter - 1, quarter)}
    next_tile = {"gx": lax.rem(own + 1, n)}
    prev_tile = {"gx": lax.rem(own + n - 1, n)}
    next_col = {"gy": lax.rem(col + 1, m)}
    prev_col = {"gy": lax.rem(col + m - 1, m)}

    barrier = pltpu.get_barrier_semaphore()
    partners = [far(1), far(2), far(3), next_group, prev_group, next_tile, prev_tile, next_col, prev_col]
    for partner in partners:
        pl.semaphore_signal(barrier, inc=1, device_id=partner, device_id_type=MESH)
    pl.semaphore_wait(barrier, len(partners))

    count = [0]
    sent = []

    def send(src, dst, device):
        at = count[0]
        count[0] += 1
        copy = pltpu.make_async_remote_copy(
            src_ref=src, dst_ref=dst, send_sem=send_sem.at[at], recv_sem=recv_sem.at[at],
            device_id=device, device_id_type=MESH,
        )
        copy.start()
        sent.append(copy)
        return copy

    def head_cols(head):
        return pl.ds(pl.multiple_of(head * HD, HD), HD)

    order = (2, 1, 3)
    arrays = ((k_ref, lambda h, s: kk.at[h, 0, s]), (v_ref, lambda h, s: vv.at[h, 0, s]),
              (q_ref, lambda h, s: qg.at[h, s]), (g_ref, lambda h, s: gg.at[h, s]))
    edge_copies = []
    for a, ref in enumerate((v_ref, g_ref)):
        edge_copies.append(send(ref.at[pl.ds(tx - 1, 1)], edge.at[a, pl.ds(0, 1)], next_tile))
        edge_copies.append(send(ref.at[pl.ds(0, 1)], edge.at[a, pl.ds(1, 1)], prev_tile))
    incoming = {}
    locals_ = []
    for h in range(hp):
        for a, (ref, place) in enumerate(arrays):
            for d in order:
                target = lax.rem(slot + d, 4)
                incoming[h, a, d] = send(ref.at[:, :, head_cols(target * hp + h)], place(h, slot), far(d))
            mine = pltpu.make_async_copy(
                ref.at[:, :, head_cols(slot * hp + h)], place(h, slot), local_sem.at[h * 4 + a])
            mine.start()
            locals_.append(mine)
        if h == 0:
            bias_copies = [send(bias_ref, bias_g.at[slot], far(d)) for d in order]
            mine = pltpu.make_async_copy(bias_ref, bias_g.at[slot], local_sem.at[hp * 4])
            mine.start()
            locals_.append(mine)
    slab_copies = []
    for a, ref in enumerate((v_ref, g_ref)):
        slab_copies.append(send(ref.at[:, pl.ds(ty - 16, 16)], slab.at[a, 0, pl.ds(1, tx)], next_col))
        slab_copies.append(send(ref.at[:, pl.ds(0, 16)], slab.at[a, 1, pl.ds(1, tx)], prev_col))
    for mine in locals_:
        mine.wait()

    forwards = {}

    def forward(h, d):
        s = lax.rem(slot + 4 - d, 4)
        for a, buf in enumerate((kk, vv)):
            if d:
                incoming[h, a, d].wait_recv()
            forwards[h, a, d, 1] = send(buf.at[h, 0, s], buf.at[h, 1, s], prev_group)
            forwards[h, a, d, 2] = send(buf.at[h, 0, s], buf.at[h, 2, s], next_group)

    for h in range(hp):
        forward(h, 0)
    for copy in edge_copies:
        copy.wait_recv()
    for a in range(2):
        for x, e in ((0, 0), (tx + 1, 1)):
            slab_copies.append(send(edge.at[a, pl.ds(e, 1), pl.ds(ty - 16, 16)], slab.at[a, 0, pl.ds(x, 1)], next_col))
            slab_copies.append(send(edge.at[a, pl.ds(e, 1), pl.ds(0, 16)], slab.at[a, 1, pl.ds(x, 1)], prev_col))
    for d in (1, 3, 2):
        forward(0, d)

    for copy in slab_copies:
        copy.wait_recv()
    has_up = (own > 0).astype(F32)
    has_down = (own < n - 1).astype(F32)
    has_left = (col > 0).astype(F32)
    has_right = (col < m - 1).astype(F32)
    for a, ref in enumerate((v_ref, g_ref)):

        @pl.loop(0, heads)
        def _(c, a=a, ref=ref):
            cols = head_cols(c)
            row_id = lax.broadcasted_iota(jnp.int32, (ty, HD), 0)
            sums = [None] * tx
            for x in range(tx + 2):
                if x == 0:
                    row = edge[a, 0, :, cols].astype(F32) * has_up
                elif x == tx + 1:
                    row = edge[a, 1, :, cols].astype(F32) * has_down
                else:
                    row = ref[x - 1, :, cols].astype(F32)
                left = slab[a, 0, x, :, cols].astype(F32)[15:16] * has_left
                right = slab[a, 1, x, :, cols].astype(F32)[0:1] * has_right
                if x == 0:
                    left, right = left * has_up, right * has_up
                if x == tx + 1:
                    left, right = left * has_down, right * has_down
                shifted = (
                    jnp.where(row_id == 0, left, pltpu.roll(row, 1, 0)),
                    row,
                    jnp.where(row_id == ty - 1, right, pltpu.roll(row, ty - 1, 0)),
                )
                for step in (-1, 0, 1):
                    target = x - 1 - step
                    if 0 <= target < tx:
                        for b in range(3):
                            tap = 3 * (step + 1) + b
                            tap = tap if a == 0 else 8 - tap
                            term = w_ref[pl.ds(tap, 1), cols] * shifted[b]
                            sums[target] = term if sums[target] is None else sums[target] + term
            for x in range(tx):
                conv[a, x, :, cols] = sums[x]

    for h in range(1, hp):
        for d in (1, 3, 2):
            forward(h, d)
    for copy in bias_copies:
        copy.wait_recv()

    ahead = (rank == quarter - 1).astype(jnp.int32)
    behind = 3 * (rank == 0).astype(jnp.int32)
    nt = (((1,), (1,)), ((), ()))
    nn = (((1,), (0,)), ((), ()))
    tn = (((0,), (0,)), ((), ()))

    def dot(x, y, dims):
        return lax.dot_general(x, y, dims, preferred_element_type=F32)

    def flat(x):
        return x.reshape(tokens, HD)

    def attend(h):
        dk_acc[h] = jnp.zeros(dk_acc.shape[1:], F32)
        dv_acc[h] = jnp.zeros(dv_acc.shape[1:], F32)

        @pl.loop(0, 4)
        def _(i):
            q = flat(qg[h, i])
            g = flat(gg[h, i])
            keys = [(0, 0), (0, 1), (0, 2), (0, 3), (1, lax.rem(i + ahead, 4)), (2, lax.rem(i + behind, 4))]
            top = None
            for j, (nb, s) in enumerate(keys):
                js = pl.ds(j * tokens, tokens)
                score = dot(q, flat(kk[h, nb, s]), nt)
                bias = bias_g[i, :, js]
                parts = [score[b * BLOCK:(b + 1) * BLOCK] + bias[b:b + 1] for b in range(tokens // BLOCK)]
                score = jnp.concatenate(parts, axis=0)
                s_sc[:, js] = score
                peak = jnp.max(score, axis=1, keepdims=True)
                top = peak if top is None else jnp.maximum(top, peak)
            total = jnp.zeros((tokens, 1), F32)
            out = jnp.zeros((tokens, HD), F32)
            for j, (nb, s) in enumerate(keys):
                js = pl.ds(j * tokens, tokens)
                prob = jnp.exp2((s_sc[:, js] - top) * (SCALE * LOG2E))
                s_sc[:, js] = prob
                total = total + jnp.sum(prob, axis=1, keepdims=True)
                out = out + dot(prob.astype(BF16), flat(vv[h, nb, s]), nn)
            inv = 1.0 / total
            out = out * inv
            res[0, h, i] = out.astype(BF16).reshape(tx, ty, HD)
            grad_dot = jnp.sum(g.astype(F32) * out, axis=1, keepdims=True)
            dq = jnp.zeros((tokens, HD), F32)
            for j, (nb, s) in enumerate(keys):
                js = pl.ds(j * tokens, tokens)
                prob_grad = dot(g, flat(vv[h, nb, s]), nt)
                prob = s_sc[:, js] * inv
                score_grad = (prob * (prob_grad - grad_dot)).astype(BF16)
                dq = dq + dot(score_grad, flat(kk[h, nb, s]), nn)
                dk = dot(score_grad, q, tn)
                dv = dot(prob.astype(BF16), g, tn)
                if nb == 0:
                    dk_acc[h, s] += dk
                    dv_acc[h, s] += dv
                else:
                    part_send[0, h, nb - 1, s] = dk.astype(BF16).reshape(tx, ty, HD)
                    part_send[1, h, nb - 1, s] = dv.astype(BF16).reshape(tx, ty, HD)
            res[1, h, i] = (dq * SCALE).astype(BF16).reshape(tx, ty, HD)

    back = []

    def give_back(a, h):
        for d in order:
            target = lax.rem(slot + d, 4)
            back.append(send(res.at[a, h, target], ret.at[a, slot * hp + h], far(d)))

    parts = {}

    def work(h):
        for d in order:
            for a in (2, 3):
                incoming[h, a, d].wait_recv()
        for a in range(2):
            for d in range(4):
                for nb in (1, 2):
                    forwards[h, a, d, nb].wait_recv()
        attend(h)
        parts[h] = [
            send(part_send.at[a, h, nb], part_recv.at[a, h, nb], (next_group, prev_group)[nb])
            for a in range(2) for nb in range(2)
        ]
        for a in (0, 1):
            give_back(a, h)

    def finish(h):
        for copy in parts[h]:
            copy.wait_recv()
        for a, acc in enumerate((dk_acc, dv_acc)):
            for s in range(4):
                value = acc[h, s] + flat(part_recv[a, h, 0, s]).astype(F32) + flat(part_recv[a, h, 1, s]).astype(F32)
                if a == 0:
                    value = value * SCALE
                res[2 + a, h, s] = value.astype(BF16).reshape(tx, ty, HD)
            give_back(2 + a, h)

    for h in range(hp):
        work(h)
    for h in range(hp):
        finish(h)
    for a in range(4):
        for h in range(hp):
            ret[a, slot * hp + h] = res[a, h, slot]
    for copy in back:
        copy.wait_recv()
    for c in range(heads):
        cols = pl.ds(c * HD, HD)
        o_ref[:, :, cols] = (ret[0, c].astype(F32) + conv[0, :, :, cols]).astype(BF16)
        dq_ref[:, :, cols] = ret[1, c]
        dk_ref[:, :, cols] = ret[2, c]
        dv_ref[:, :, cols] = (ret[3, c].astype(F32) + conv[1, :, :, cols]).astype(BF16)
    for copy in sent:
        copy.wait_send()


def bias_rows(block_pairs, n, tokens):
    quarter = n // 4
    own = lax.axis_index("gx")
    rank = own % quarter
    blocks = tokens // BLOCK
    tiles = jnp.concatenate([
        rank + quarter * jnp.arange(4, dtype=jnp.int32),
        jnp.stack([(own + 1) % n, (own + n - 1) % n]).astype(jnp.int32),
    ])
    key_at = jnp.repeat(tiles, tokens) * blocks + jnp.tile(jnp.arange(tokens, dtype=jnp.int32) // BLOCK, 6)
    query = jnp.arange(8, dtype=jnp.int32)
    pairs = block_pairs[0, 0]
    listed = (pairs[:, 0][:, None, None] == query[None, :, None]) & (pairs[:, 1][:, None, None] == key_at[None, None, :])
    allowed = jnp.any(listed, axis=0) | ((own * blocks + query)[:, None] == key_at[None, :])
    return jnp.where(allowed, 0.0, NEG).astype(F32)


def per_device(n, m, queries, key_tokens, value_tokens, out_grad, conv_weight, block_pairs):
    tx, ty, width = queries.shape
    heads = width // HD
    hp = heads // 4
    tokens = tx * ty
    bias = bias_rows(block_pairs, n, tokens)
    vmem = pl.BlockSpec(memory_space=pltpu.VMEM)
    shape = jax.ShapeDtypeStruct(queries.shape, BF16)
    return pl.pallas_call(
        functools.partial(kernel, n, m, tx, ty),
        out_shape=(shape,) * 4,
        in_specs=[vmem] * 6,
        out_specs=(vmem,) * 4,
        scratch_shapes=[
            pltpu.VMEM((hp, 4, tx, ty, HD), BF16),
            pltpu.VMEM((hp, 4, tx, ty, HD), BF16),
            pltpu.VMEM((hp, 3, 4, tx, ty, HD), BF16),
            pltpu.VMEM((hp, 3, 4, tx, ty, HD), BF16),
            pltpu.VMEM((4, 8, 6 * tokens), F32),
            pltpu.VMEM((tokens, 6 * tokens), F32),
            pltpu.VMEM((hp, 4, tokens, HD), F32),
            pltpu.VMEM((hp, 4, tokens, HD), F32),
            pltpu.VMEM((2, hp, 2, 4, tx, ty, HD), BF16),
            pltpu.VMEM((2, hp, 2, 4, tx, ty, HD), BF16),
            pltpu.VMEM((4, hp, 4, tx, ty, HD), BF16),
            pltpu.VMEM((4, heads, tx, ty, HD), BF16),
            pltpu.VMEM((2, 2, ty, width), BF16),
            pltpu.VMEM((2, 2, tx + 2, 16, width), BF16),
            pltpu.VMEM((2, tx, ty, width), F32),
            pltpu.SemaphoreType.DMA((160,)),
            pltpu.SemaphoreType.DMA((160,)),
            pltpu.SemaphoreType.DMA((4 * hp + 1,)),
        ],
        compiler_params=pltpu.CompilerParams(
            collective_id=0, has_side_effects=True, vmem_limit_bytes=60 * 1024 * 1024
        ),
    )(queries, key_tokens, value_tokens, out_grad, conv_weight, bias)


def solution(mesh):
    grid = P("gx", "gy", None)
    return jax.shard_map(
        functools.partial(per_device, mesh.shape["gx"], mesh.shape["gy"]),
        mesh=mesh,
        in_specs=(grid, grid, grid, grid, P(), P("gx", "gy", None, None)),
        out_specs=(grid, grid, grid, grid),
        check_vma=False,
    )
```

time: 371 us -> 122 us (0.33)
  waiting for transfers between devices: 245 us -> 0 us
  Pallas kernels: 0 us -> 113 us
  matrix products: 39.2 us -> 0 us
  starting transfers between devices: 35.4 us -> 0 us
  local copies, waits for them, and re-layouts: 31.6 us -> 5.87 us
  other arithmetic: 11.7 us -> 1.15 us
    ppermute x28 -> x0, waiting for transfers between devices: 245 us -> none  [the longest x20 209 us: passed_along(): return lax.ppermute(value, axis, pairs)]
    pallas_call x0 -> x1, Pallas kernels: none -> 113 us  [per_device(): pl.pallas_call(functools.partial(kernel, n, m, tx, ty), out_shape=(shape,...]
    dot_general x36 -> x0, matrix products: 39.2 us -> none  [the longest x6 10.8 us: query_update(): jnp.einsum('hqk,qhd->khd', probabilities.astype(jnp.bfloat16), grad_heads...]
    ppermute x28 -> x0, starting transfers between devices: 35.4 us -> none  [the longest x20 17.2 us: passed_along(): return lax.ppermute(value, axis, pairs)]
    unnamed x172 -> x12, local copies, waits for them, and re-layouts: 15.5 us -> 5.86 us
    convert_element_type x2 -> x0, other arithmetic: 7.85 us -> none  [the longest x1 4.21 us: per_device(): (value_sum.reshape(tile_x, tile_y, width) + conv_back).astype(jnp.bfloat16)]
    slice x5 -> x1, local copies, waits for them, and re-layouts: 5.5 us -> 0.01 us  [bias_rows(): pairs[:, 0][:, None, None] == query[None, :, None]]
  transfers between devices with their start and end apart: 28 -> 0, of which waited for: 12 -> 0; matrix products, arithmetic and copies ran while one was open for 20% -> 0% of each run, Pallas kernels for 0% -> 0%
where the time goes in v1:
time: 122 us; the launch traced here: 120 us
  Pallas kernels  113 us (93%)
  local copies, waits for them, and re-layouts  5.87 us (5%)
    pallas_call x1, Pallas kernels, per_device(): pl.pallas_call(functools.partial(kernel, n, m, tx, ty), out_shape=(shape,...  113 us
    unnamed x12, local copies, waits for them, and re-layouts  5.86 us

profile of v1, /device:TPU:15, one launch (start us, length us, event | category | flops | bytes accessed | tf_op | source)
XLA Modules:
  0.0 120.5 jit_solution(5750572400709121551)
XLA Ops:
  0.7 0.1 add_multiply_fusion
  0.8 0.0 copy-start.3
  0.8 0.7 copy-done.3
  1.4 0.1 iota_compare_fusion
  1.5 0.1 broadcast_add_fusion
  1.6 0.1 broadcast_compare_fusion
  1.7 0.1 and_reduce_fusion
  1.8 0.7 or_select_fusion.bias_ref
  2.5 112.8 %shard_map.93 = (bf16[4,64,1024]{2,1,0:T(8,128)(2,1)}, bf16[4,64,1024]{2,1,0:T(8,128)(2,1)}, bf16[4,64,1024]{2,1,0:T(8,128)(2,1)}, bf16[4,64,1024]{2,1,0:T(8,128)(2,1)}) custom-call(bf16[4,64,1024]{2,1,0:T(8,128)(2,1)} %q_ref.1, bf16[4,64,1024]{2,1,0:T(8,128)(2,1)} %k_ref.1, bf16[4,64,1024]{2,1,0:T(8,128)(2,1)} %v_ref.1, bf16[4,64,1024]{2,1,0:T(8,128)(2,1)} %g_ref.1, ...), custom_call_target="tpu_custom_call" | custom-call | tf_op jit(solution)/shard_map/pallas_call | solution.py:310
  115.3 0.0 copy-start.2
  115.3 1.9 %copy.14 = bf16[4,64,1024]{2,1,0:T(8,128)(2,1)} copy(bf16[4,64,1024]{2,1,0:T(8,128)(2,1)} %get-tuple-element.10) | data formatting | bytes 1048576
  117.2 0.0 copy-done.2
  117.2 0.0 copy-start.1
  117.2 0.8 copy.15
  118.0 0.4 copy-done.1
  118.5 0.0 copy-start
  118.5 0.8 copy.16
  119.3 0.4 copy-done
  119.7 0.8 copy.17
  (5 shorter events, 0.0 us)
Async XLA Ops:
  0.8 0.7 copy-start.3
  115.3 1.9 %copy-start.2 = (bf16[4,64,1024]{2,1,0:T(8,128)(2,1)S(1)}, bf16[4,64,1024]{2,1,0:T(8,128)(2,1)}, u32[]{:S(2)}) copy-start(bf16[4,64,1024]{2,1,0:T(8,128)(2,1)} %get-tuple-element.11) | copy-start | bytes 1572868
  117.2 1.2 %copy-start.1 = (bf16[4,64,1024]{2,1,0:T(8,128)(2,1)S(1)}, bf16[4,64,1024]{2,1,0:T(8,128)(2,1)}, u32[]{:S(2)}) copy-start(bf16[4,64,1024]{2,1,0:T(8,128)(2,1)} %get-tuple-element.12) | copy-start | bytes 1572868
  118.5 1.2 %copy-start = (bf16[4,64,1024]{2,1,0:T(8,128)(2,1)S(1)}, bf16[4,64,1024]{2,1,0:T(8,128)(2,1)}, u32[]{:S(2)}) copy-start(bf16[4,64,1024]{2,1,0:T(8,128)(2,1)} %get-tuple-element.13) | copy-start | bytes 1572868

commit v2 on v1

--- a/solution.py
+++ b/solution.py
@@ -65,16 +65,32 @@
         sent.append(copy)
         return copy
 
+    edge_copies = []
+
+    def edge_send(src, dst, device, sends, receives):
+        at = count[0]
+        count[0] += 1
+        copy = pltpu.make_async_remote_copy(
+            src_ref=src, dst_ref=dst, send_sem=send_sem.at[at], recv_sem=recv_sem.at[at],
+            device_id=device, device_id_type=MESH,
+        )
+
+        @pl.when(sends)
+        def _():
+            copy.start()
+
+        @pl.when(jnp.logical_not(receives))
+        def _():
+            dst[...] = jnp.zeros(dst.shape, BF16)
+
+        edge_copies.append((copy, sends, receives))
+
     def head_cols(head):
         return pl.ds(pl.multiple_of(head * HD, HD), HD)
 
     order = (2, 1, 3)
     arrays = ((k_ref, lambda h, s: kk.at[h, 0, s]), (v_ref, lambda h, s: vv.at[h, 0, s]),
               (q_ref, lambda h, s: qg.at[h, s]), (g_ref, lambda h, s: gg.at[h, s]))
-    edge_copies = []
-    for a, ref in enumerate((v_ref, g_ref)):
-        edge_copies.append(send(ref.at[pl.ds(tx - 1, 1)], edge.at[a, pl.ds(0, 1)], next_tile))
-        edge_copies.append(send(ref.at[pl.ds(0, 1)], edge.at[a, pl.ds(1, 1)], prev_tile))
     incoming = {}
     locals_ = []
     for h in range(hp):
@@ -87,6 +103,9 @@
             mine.start()
             locals_.append(mine)
         if h == 0:
+            for a, ref in enumerate((v_ref, g_ref)):
+                edge_send(ref.at[pl.ds(tx - 1, 1)], edge.at[a, pl.ds(0, 1)], next_tile, own < n - 1, own > 0)
+                edge_send(ref.at[pl.ds(0, 1)], edge.at[a, pl.ds(1, 1)], prev_tile, own > 0, own < n - 1)
             bias_copies = [send(bias_ref, bias_g.at[slot], far(d)) for d in order]
             mine = pltpu.make_async_copy(bias_ref, bias_g.at[slot], local_sem.at[hp * 4])
             mine.start()
@@ -110,8 +129,8 @@
 
     for h in range(hp):
         forward(h, 0)
-    for copy in edge_copies:
-        copy.wait_recv()
+    for copy, _, receives in edge_copies:
+        pl.when(receives)(copy.wait_recv)
     for a in range(2):
         for x, e in ((0, 0), (tx + 1, 1)):
             slab_copies.append(send(edge.at[a, pl.ds(e, 1), pl.ds(ty - 16, 16)], slab.at[a, 0, pl.ds(x, 1)], next_col))
@@ -227,12 +246,12 @@
                     part_send[1, h, nb - 1, s] = dv.astype(BF16).reshape(tx, ty, HD)
             res[1, h, i] = (dq * SCALE).astype(BF16).reshape(tx, ty, HD)
 
-    back = []
+    back = {0: [], 1: [], 2: [], 3: []}
 
     def give_back(a, h):
         for d in order:
             target = lax.rem(slot + d, 4)
-            back.append(send(res.at[a, h, target], ret.at[a, slot * hp + h], far(d)))
+            back[a].append(send(res.at[a, h, target], ret.at[a, slot * hp + h], far(d)))
 
     parts = {}
 
@@ -244,6 +263,8 @@
             for d in range(4):
                 for nb in (1, 2):
                     forwards[h, a, d, nb].wait_recv()
+        if h:
+            finish(h - 1)
         attend(h)
         parts[h] = [
             send(part_send.at[a, h, nb], part_recv.at[a, h, nb], (next_group, prev_group)[nb])
@@ -265,21 +286,23 @@
 
     for h in range(hp):
         work(h)
-    for h in range(hp):
-        finish(h)
+    finish(hp - 1)
+    outputs = (o_ref, dq_ref, dk_ref, dv_ref)
     for a in range(4):
         for h in range(hp):
             ret[a, slot * hp + h] = res[a, h, slot]
-    for copy in back:
-        copy.wait_recv()
-    for c in range(heads):
-        cols = pl.ds(c * HD, HD)
-        o_ref[:, :, cols] = (ret[0, c].astype(F32) + conv[0, :, :, cols]).astype(BF16)
-        dq_ref[:, :, cols] = ret[1, c]
-        dk_ref[:, :, cols] = ret[2, c]
-        dv_ref[:, :, cols] = (ret[3, c].astype(F32) + conv[1, :, :, cols]).astype(BF16)
+        for copy in back[a]:
+            copy.wait_recv()
+        for c in range(heads):
+            cols = pl.ds(c * HD, HD)
+            if a in (0, 3):
+                outputs[a][:, :, cols] = (ret[a, c].astype(F32) + conv[a // 3, :, :, cols]).astype(BF16)
+            else:
+                outputs[a][:, :, cols] = ret[a, c]
     for copy in sent:
         copy.wait_send()
+    for copy, sends, _ in edge_copies:
+        pl.when(sends)(copy.wait_send)
 
 
 def bias_rows(block_pairs, n, tokens):

time: 122 us -> 121 us (level)
  no operation moved by 1% of the time
where the time goes in v2:
time: 121 us; the launch traced here: 120 us
  Pallas kernels  112 us (93%)
  local copies, waits for them, and re-layouts  5.87 us (5%)
    pallas_call x1, Pallas kernels, per_device(): pl.pallas_call(functools.partial(kernel, n, m, tx, ty), out_shape=(shape,...  112 us
    unnamed x12, local copies, waits for them, and re-layouts  5.86 us

profile of v2, /device:TPU:15, one launch (start us, length us, event | category | flops | bytes accessed | tf_op | source)
XLA Modules:
  0.0 119.9 jit_solution(15984031783679389143)
XLA Ops:
  0.7 0.1 add_multiply_fusion
  0.8 0.0 copy-start.3
  0.8 0.7 copy-done.3
  1.4 0.1 iota_compare_fusion
  1.5 0.1 broadcast_add_fusion
  1.6 0.1 broadcast_compare_fusion
  1.7 0.1 and_reduce_fusion
  1.8 0.7 or_select_fusion.bias_ref
  2.5 112.2 %shard_map.93 = (bf16[4,64,1024]{2,1,0:T(8,128)(2,1)}, bf16[4,64,1024]{2,1,0:T(8,128)(2,1)}, bf16[4,64,1024]{2,1,0:T(8,128)(2,1)}, bf16[4,64,1024]{2,1,0:T(8,128)(2,1)}) custom-call(bf16[4,64,1024]{2,1,0:T(8,128)(2,1)} %q_ref.1, bf16[4,64,1024]{2,1,0:T(8,128)(2,1)} %k_ref.1, bf16[4,64,1024]{2,1,0:T(8,128)(2,1)} %v_ref.1, bf16[4,64,1024]{2,1,0:T(8,128)(2,1)} %g_ref.1, ...), custom_call_target="tpu_custom_call" | custom-call | tf_op jit(solution)/shard_map/pallas_call | solution.py:333
  114.7 0.0 copy-start.2
  114.7 1.9 %copy.14 = bf16[4,64,1024]{2,1,0:T(8,128)(2,1)} copy(bf16[4,64,1024]{2,1,0:T(8,128)(2,1)} %get-tuple-element.10) | data formatting | bytes 1048576
  116.7 0.0 copy-done.2
  116.7 0.0 copy-start.1
  116.7 0.8 copy.15
  117.5 0.4 copy-done.1
  117.9 0.0 copy-start
  117.9 0.8 copy.16
  118.7 0.4 copy-done
  119.1 0.8 copy.17
  (5 shorter events, 0.0 us)
Async XLA Ops:
  0.8 0.7 copy-start.3
  114.7 1.9 %copy-start.2 = (bf16[4,64,1024]{2,1,0:T(8,128)(2,1)S(1)}, bf16[4,64,1024]{2,1,0:T(8,128)(2,1)}, u32[]{:S(2)}) copy-start(bf16[4,64,1024]{2,1,0:T(8,128)(2,1)} %get-tuple-element.11) | copy-start | bytes 1572868
  116.7 1.2 %copy-start.1 = (bf16[4,64,1024]{2,1,0:T(8,128)(2,1)S(1)}, bf16[4,64,1024]{2,1,0:T(8,128)(2,1)}, u32[]{:S(2)}) copy-start(bf16[4,64,1024]{2,1,0:T(8,128)(2,1)} %get-tuple-element.12) | copy-start | bytes 1572868
  117.9 1.2 %copy-start = (bf16[4,64,1024]{2,1,0:T(8,128)(2,1)S(1)}, bf16[4,64,1024]{2,1,0:T(8,128)(2,1)}, u32[]{:S(2)}) copy-start(bf16[4,64,1024]{2,1,0:T(8,128)(2,1)} %get-tuple-element.13) | copy-start | bytes 1572868

commit v3 on v2

--- a/solution.py
+++ b/solution.py
@@ -198,11 +198,12 @@
     def flat(x):
         return x.reshape(tokens, HD)
 
-    def attend(h):
-        dk_acc[h] = jnp.zeros(dk_acc.shape[1:], F32)
-        dv_acc[h] = jnp.zeros(dv_acc.shape[1:], F32)
-
-        @pl.loop(0, 4)
+    def attend(h, first, last):
+        if first == 0:
+            dk_acc[h] = jnp.zeros(dk_acc.shape[1:], F32)
+            dv_acc[h] = jnp.zeros(dv_acc.shape[1:], F32)
+
+        @pl.loop(first, last)
         def _(i):
             q = flat(qg[h, i])
             g = flat(gg[h, i])
@@ -265,18 +266,23 @@
                     forwards[h, a, d, nb].wait_recv()
         if h:
             finish(h - 1)
-        attend(h)
-        parts[h] = [
-            send(part_send.at[a, h, nb], part_recv.at[a, h, nb], (next_group, prev_group)[nb])
-            for a in range(2) for nb in range(2)
-        ]
+        parts[h] = {0: [], 1: []}
+        width = 4 if h < hp - 1 else 2
+        for first in range(0, 4, width):
+            attend(h, first, first + width)
+            for a in range(2):
+                for i in range(first, first + width):
+                    for nb, shift in ((0, ahead), (1, behind)):
+                        at = (a, h, nb, lax.rem(i + shift, 4))
+                        parts[h][a].append(
+                            send(part_send.at[at], part_recv.at[at], (next_group, prev_group)[nb]))
         for a in (0, 1):
             give_back(a, h)
 
     def finish(h):
-        for copy in parts[h]:
-            copy.wait_recv()
         for a, acc in enumerate((dk_acc, dv_acc)):
+            for copy in parts[h][a]:
+                copy.wait_recv()
             for s in range(4):
                 value = acc[h, s] + flat(part_recv[a, h, 0, s]).astype(F32) + flat(part_recv[a, h, 1, s]).astype(F32)
                 if a == 0:

time: 121 us -> 121 us (level)
  no operation moved by 1% of the time
where the time goes in v3:
time: 121 us; the launch traced here: 120 us
  Pallas kernels  112 us (93%)
  local copies, waits for them, and re-layouts  5.87 us (5%)
    pallas_call x1, Pallas kernels, per_device(): pl.pallas_call(functools.partial(kernel, n, m, tx, ty), out_shape=(shape,...  112 us
    unnamed x12, local copies, waits for them, and re-layouts  5.86 us

profile of v3, /device:TPU:15, one launch (start us, length us, event | category | flops | bytes accessed | tf_op | source)
XLA Modules:
  0.0 120.0 jit_solution(8771624613801456033)
XLA Ops:
  0.7 0.1 add_multiply_fusion
  0.8 0.0 copy-start.3
  0.8 0.7 copy-done.3
  1.4 0.1 iota_compare_fusion
  1.5 0.1 broadcast_add_fusion
  1.6 0.1 broadcast_compare_fusion
  1.7 0.1 and_reduce_fusion
  1.8 0.7 or_select_fusion.bias_ref
  2.5 112.3 %shard_map.93 = (bf16[4,64,1024]{2,1,0:T(8,128)(2,1)}, bf16[4,64,1024]{2,1,0:T(8,128)(2,1)}, bf16[4,64,1024]{2,1,0:T(8,128)(2,1)}, bf16[4,64,1024]{2,1,0:T(8,128)(2,1)}) custom-call(bf16[4,64,1024]{2,1,0:T(8,128)(2,1)} %q_ref.1, bf16[4,64,1024]{2,1,0:T(8,128)(2,1)} %k_ref.1, bf16[4,64,1024]{2,1,0:T(8,128)(2,1)} %v_ref.1, bf16[4,64,1024]{2,1,0:T(8,128)(2,1)} %g_ref.1, ...), custom_call_target="tpu_custom_call" | custom-call | tf_op jit(solution)/shard_map/pallas_call | solution.py:339
  114.8 0.0 copy-start.2
  114.8 1.9 %copy.14 = bf16[4,64,1024]{2,1,0:T(8,128)(2,1)} copy(bf16[4,64,1024]{2,1,0:T(8,128)(2,1)} %get-tuple-element.10) | data formatting | bytes 1048576
  116.7 0.0 copy-done.2
  116.7 0.0 copy-start.1
  116.7 0.8 copy.15
  117.5 0.4 copy-done.1
  118.0 0.0 copy-start
  118.0 0.8 copy.16
  118.8 0.4 copy-done
  119.2 0.8 copy.17
  (5 shorter events, 0.0 us)
Async XLA Ops:
  0.8 0.7 copy-start.3
  114.8 1.9 %copy-start.2 = (bf16[4,64,1024]{2,1,0:T(8,128)(2,1)S(1)}, bf16[4,64,1024]{2,1,0:T(8,128)(2,1)}, u32[]{:S(2)}) copy-start(bf16[4,64,1024]{2,1,0:T(8,128)(2,1)} %get-tuple-element.11) | copy-start | bytes 1572868
  116.7 1.2 %copy-start.1 = (bf16[4,64,1024]{2,1,0:T(8,128)(2,1)S(1)}, bf16[4,64,1024]{2,1,0:T(8,128)(2,1)}, u32[]{:S(2)}) copy-start(bf16[4,64,1024]{2,1,0:T(8,128)(2,1)} %get-tuple-element.12) | copy-start | bytes 1572868
  118.0 1.2 %copy-start = (bf16[4,64,1024]{2,1,0:T(8,128)(2,1)S(1)}, bf16[4,64,1024]{2,1,0:T(8,128)(2,1)}, u32[]{:S(2)}) copy-start(bf16[4,64,1024]{2,1,0:T(8,128)(2,1)} %get-tuple-element.13) | copy-start | bytes 1572868
